TPU v7x, 32 devices: a whole 2x2x4 slice. The times are simulated.
32 devices in a mesh: groups: 2 (over y), tensor: 4 (over z), dp: 4 (over x, core).
Axes of the slice: x: 2, y: 2, z: 4, core: 2. Of those that a mesh axis runs over, the one named last changes fastest.
Arguments:
- tokens: bfloat16 [256, 8192], P(('groups', 'tensor', 'dp')), parts along dimension 0, may hold values from -6 to 6
- gate_projection_matrix: bfloat16 [8192, 14336], P('dp', 'tensor'), may hold values from -0.0625 to 0.0625
- up_projection_matrix: bfloat16 [8192, 14336], P('dp', 'tensor'), may hold values from -0.0625 to 0.0625
- down_projection_matrix: bfloat16 [14336, 8192], P('tensor', 'dp'), may hold values from -0.046875 to 0.046875
- gate_adapter_inmap: bfloat16 [16384, 64], P(('groups', 'dp')), parts along dimension 0, may hold values from -0.0625 to 0.0625
- gate_adapter_outmap: bfloat16 [64, 28672], P(None, ('groups', 'tensor')), parts along dimension 1, may hold values from -0.75 to 0.75
- up_adapter_inmap: bfloat16 [16384, 64], P(('groups', 'dp')), parts along dimension 0, may hold values from -0.0625 to 0.0625
- up_adapter_outmap: bfloat16 [64, 28672], P(None, ('groups', 'tensor')), parts along dimension 1, may hold values from -0.75 to 0.75
- down_adapter_inmap: bfloat16 [28672, 64], P(('groups', 'tensor')), parts along dimension 0, may hold values from -0.046875 to 0.046875
- down_adapter_outmap: bfloat16 [64, 16384], P(None, 'groups'), parts along dimension 1, may hold values from -0.75 to 0.75
Outputs:
- block_out: bfloat16 [256, 8192], P(('groups', 'tensor', 'dp')), parts along dimension 0
There are 2 independent parts, one for each index of `groups`. A program takes and returns all parts, laid end to end along the dimension named above; an argument that names none is the same for every part. Nothing has to cross between parts.
All inputs are finite; a program needn't handle non-finite values.
Results may differ from a plain program's by a relative error of at most 0.0053.
Values may be sent and summed in bfloat16 or wider, within the bound.
A program may use at most 256 MiB of HBM per device.

v0:
```python
import jax
import jax.numpy as jnp
from jax import lax
from jax.sharding import PartitionSpec as P

adapter_scale_factor = 0.5


def body(
    tokens,
    gate_projection_matrix,
    up_projection_matrix,
    down_projection_matrix,
    gate_adapter_inmap,
    gate_adapter_outmap,
    up_adapter_inmap,
    up_adapter_outmap,
    down_adapter_inmap,
    down_adapter_outmap,
):
    adapter_rank_size = gate_adapter_inmap.shape[1]
    columns = lax.all_to_all(tokens, "dp", split_axis=1, concat_axis=0, tiled=True)
    gathered = lax.all_gather(columns, "tensor", axis=0, tiled=True)

    def summed(weights):
        partial = jnp.dot(gathered, weights, preferred_element_type=jnp.float32)
        return lax.psum_scatter(partial, "dp", scatter_dimension=0, tiled=True)

    gate_dense_part = summed(gate_projection_matrix)
    up_dense_part = summed(up_projection_matrix)
    lowrank = summed(jnp.concatenate([gate_adapter_inmap, up_adapter_inmap], axis=1)).astype(
        jnp.bfloat16
    )
    gate_lowrank_part = lowrank[:, :adapter_rank_size]
    up_lowrank_part = lowrank[:, adapter_rank_size:]
    gate_activated = gate_dense_part + adapter_scale_factor * jnp.dot(
        gate_lowrank_part, gate_adapter_outmap, preferred_element_type=jnp.float32
    )
    up_projected_value = up_dense_part + adapter_scale_factor * jnp.dot(
        up_lowrank_part, up_adapter_outmap, preferred_element_type=jnp.float32
    )
    hidden_product = (jax.nn.silu(gate_activated) * up_projected_value).astype(jnp.bfloat16)
    hidden_all = lax.all_gather(hidden_product, "dp", axis=0, tiled=True)
    low = jnp.dot(hidden_all, down_adapter_inmap, preferred_element_type=jnp.float32)
    width = down_projection_matrix.shape[1]
    own_map = lax.dynamic_slice_in_dim(
        down_adapter_outmap, lax.axis_index("dp") * width, width, axis=1
    ).astype(jnp.float32)
    term = jnp.dot(hidden_all, down_projection_matrix, preferred_element_type=jnp.float32)
    term = term + adapter_scale_factor * jnp.dot(low, own_map, precision=lax.Precision.HIGHEST)
    rows_out = lax.psum_scatter(term, "tensor", scatter_dimension=0, tiled=True)
    return lax.all_to_all(
        rows_out.astype(jnp.bfloat16), "dp", split_axis=0, concat_axis=1, tiled=True
    )


def solution(mesh):
    placed = (
        P(("groups", "tensor", "dp"), None),
        P("dp", "tensor"),
        P("dp", "tensor"),
        P("tensor", "dp"),
        P(("groups", "dp"), None),
        P(None, ("groups", "tensor")),
        P(("groups", "dp"), None),
        P(None, ("groups", "tensor")),
        P(("groups", "tensor"), None),
        P(None, "groups"),
    )
    return jax.shard_map(
        body,
        mesh=mesh,
        in_specs=placed,
        out_specs=P(("groups", "tensor", "dp"), None),
        check_vma=False,
    )
```

profile of v0, /device:TPU:0, one launch (start us, length us, event | category | flops | bytes accessed | tf_op | source)
XLA Modules:
  0.0 181.7 jit_solution(13152078661154141634)
XLA Ops:
  6.5 0.0 copy-start
  6.5 0.0 reduce-scatter.13.cloned.1.call-start
  6.5 9.0 %all_to_all.38 = bf16[8,4,2048]{2,0,1:T(8,128)(2,1)S(1)} all-to-all(bf16[8,4,2048]{2,0,1:T(8,128)(2,1)} %bitcast.26), channel_id=1, replica_groups=mesh['groups'=2,'tensor'=4,'dp'=4] {'dp'}, dimensions={1} | all-to-all | bytes 262144 | tf_op jit(solution)/shard_map/all_to_all | solution.py:22
  15.5 16.2 %all_gather.6 = bf16[128,2048]{1,0:T(8,128)(2,1)S(1)} all-gather(bf16[32,2048]{1,0:T(8,128)(2,1)S(1)} %bitcast.24), channel_id=1, replica_groups=mesh['groups'=2,'tensor'=4,'dp'=4] {'tensor'}, dimensions={0}, use_global_device_ids=true | all-gather | bytes 655360 | tf_op jit(solution)/shard_map/all_gather | solution.py:23
  31.7 1.3 convolution_bitcast_fusion
  33.0 0.7 copy.11
  33.7 0.0 reduce-scatter.13.cloned.1.call-update
  33.8 0.0 reduce-scatter.7.cloned.1.call-start
  33.8 8.5 %fusion.13 = f32[128,3584]{1,0:T(8,128)} fusion(bf16[128,2048]{1,0:T(8,128)(2,1)S(1)} %all_gather.6, bf16[2048,3584]{1,0:T(8,128)(2,1)} %param.11), kind=kOutput, calls=%fused_computation.18 | convolution fusion | flops 1879048192 | bytes 17039360 | tf_op jit(solution)/shard_map/dot_general | solution.py:26
  42.3 0.0 copy-start.2
  42.3 0.0 copy-start.3
  42.3 0.0 reduce-scatter.7.cloned.1.call-update
  42.3 0.0 reduce-scatter.9.cloned.1.call-start
  42.4 8.6 %fusion.14 = f32[128,3584]{1,0:T(8,128)} fusion(bf16[128,2048]{1,0:T(8,128)(2,1)S(1)} %all_gather.6, bf16[2048,3584]{1,0:T(8,128)(2,1)} %param.12), kind=kOutput, calls=%fused_computation.19 | convolution fusion | flops 1879048192 | bytes 17039360 | tf_op jit(solution)/shard_map/dot_general | solution.py:26
  51.0 0.0 copy-start.1
  51.0 0.0 reduce-scatter.9.cloned.1.call-update
  51.0 0.0 reduce-scatter.11.cloned.1.call-start
  51.1 3.4 %reduce-scatter.13.cloned.1.call-done = f32[32,128]{1,0:T(8,128)} async-done(((f32[128,128]{1,0:T(8,128)}), f32[32,128]{1,0:T(8,128)}) %reduce-scatter.13.cloned.1.call-update) | async-done | bytes 16400
  54.5 0.8 copy.12
  55.3 31.4 %reduce-scatter.7.cloned.1.call-done = f32[32,3584]{1,0:T(8,128)} async-done(((f32[128,3584]{1,0:T(8,128)}), f32[32,3584]{1,0:T(8,128)}) %reduce-scatter.7.cloned.1.call-update) | async-done | bytes 458768 | tf_op jit(solution)/shard_map/reduce_scatter | solution.py:27
  86.7 0.0 copy-done.2
  86.7 1.3 fusion.2
  88.0 30.9 %reduce-scatter.9.cloned.1.call-done = f32[32,3584]{1,0:T(8,128)} async-done(((f32[128,3584]{1,0:T(8,128)}), f32[32,3584]{1,0:T(8,128)}) %reduce-scatter.9.cloned.1.call-update) | async-done | bytes 458768 | tf_op jit(solution)/shard_map/reduce_scatter | solution.py:27
  118.9 0.0 copy-done.3
  118.9 1.3 fusion.3
  120.2 8.7 %all_gather.7 = bf16[128,3584]{1,0:T(8,128)(2,1)S(1)} all-gather(bf16[32,3584]{1,0:T(8,128)(2,1)S(1)} %fusion.3), channel_id=1, replica_groups=mesh['groups'=2,'tensor'=4,'dp'=4] {'dp'}, dimensions={0}, use_global_device_ids=true | all-gather | bytes 1146880 | tf_op jit(solution)/shard_map/all_gather | solution.py:43
  128.9 7.5 %fusion.15 = f32[128,2048]{1,0:T(8,128)S(1)} fusion(bf16[128,3584]{1,0:T(8,128)(2,1)S(1)} %all_gather.7, bf16[3584,2048]{1,0:T(8,128)(2,1)} %param.13), kind=kOutput, calls=%fused_computation.20 | convolution fusion | flops 1879048192 | bytes 16646144 | tf_op jit(solution)/shard_map/dot_general | solution.py:49
  136.4 0.0 copy-done.1
  136.4 0.4 fusion.16
  136.8 0.0 copy-done
  136.8 1.6 fusion.4
  138.4 0.0 reduce-scatter.11.cloned.1.call-update
  138.4 28.0 %reduce-scatter.11.cloned.1.call-done = f32[32,2048]{1,0:T(8,128)} async-done(((f32[128,2048]{1,0:T(8,128)}), f32[32,2048]{1,0:T(8,128)}) %reduce-scatter.11.cloned.1.call-update) | async-done | bytes 262160 | tf_op jit(solution)/shard_map/reduce_scatter | solution.py:51
  166.4 1.0 convert_bitcast_fusion
  167.4 7.1 %all_to_all.39 = bf16[4,8,2048]{2,1,0:T(8,128)(2,1)S(1)} all-to-all(bf16[4,8,2048]{2,1,0:T(8,128)(2,1)S(1)} %convert_bitcast_fusion), channel_id=1, replica_groups=mesh['groups'=2,'tensor'=4,'dp'=4] {'dp'}, dimensions={0} | all-to-all | bytes 262144 | tf_op jit(solution)/shard_map/all_to_all | solution.py:52
  174.5 0.7 copy.14
Async XLA Ops:
  6.5 130.3 %copy-start = (bf16[64,8192]{1,0:T(8,128)(2,1)S(1)}, bf16[64,8192]{1,0:T(8,128)(2,1)}, u32[]{:S(2)}) copy-start(bf16[64,8192]{1,0:T(8,128)(2,1)} %param.19) | copy-start | bytes 3145732
  6.5 47.9 %reduce-scatter.13.cloned.1.call-start = ((), (), s32[]{:S(2)}) async-start(), calls=%async_computation.9 | async-start | bytes 81920
  33.8 52.9 %reduce-scatter.7.cloned.1.call-start = ((), (), s32[]{:S(2)}) async-start(), calls=%async_computation.6 | async-start | bytes 2293760 | tf_op jit(solution)/shard_map/reduce_scatter | solution.py:27
  42.3 44.4 %copy-start.2 = (bf16[64,3584]{1,0:T(8,128)(2,1)S(1)}, bf16[64,3584]{1,0:T(8,128)(2,1)}, u32[]{:S(2)}) copy-start(bf16[64,3584]{1,0:T(8,128)(2,1)} %param.15) | copy-start | bytes 1376260
  42.3 76.6 %copy-start.3 = (bf16[64,3584]{1,0:T(8,128)(2,1)S(1)}, bf16[64,3584]{1,0:T(8,128)(2,1)}, u32[]{:S(2)}) copy-start(bf16[64,3584]{1,0:T(8,128)(2,1)} %param.17) | copy-start | bytes 1376260
  42.3 76.5 %reduce-scatter.9.cloned.1.call-start = ((), (), s32[]{:S(2)}) async-start(), calls=%async_computation.7 | async-start | bytes 2293760 | tf_op jit(solution)/shard_map/reduce_scatter | solution.py:27
  51.0 85.5 %copy-start.1 = (bf16[3584,64]{0,1:T(8,128)(2,1)S(1)}, bf16[3584,64]{0,1:T(8,128)(2,1)}, u32[]{:S(2)}) copy-start(bf16[3584,64]{0,1:T(8,128)(2,1)} %param.18) | copy-start | bytes 1376260
  51.0 115.4 %reduce-scatter.11.cloned.1.call-start = ((), (), s32[]{:S(2)}) async-start(), calls=%async_computation.8 | async-start | bytes 1310720 | tf_op jit(solution)/shard_map/reduce_scatter | solution.py:51
Sparse Core Ops, SparseCore 0:
  33.9 20.5 reduce-scatter.12
  57.0 29.6 reduce-scatter.6
  89.2 29.5 reduce-scatter.8
  138.5 27.8 reduce-scatter.10
where the time goes:
time: 182 us
  waiting for transfers between devices  93.8 us (52%)
  blocking collectives  41 us (23%)
  matrix products  30.4 us (17%)
  between operations  13.2 us (7%)
  local copies, waits for them, and re-layouts  2.23 us (1%)
    reduce_scatter x2, waiting for transfers between devices, summed(): return lax.psum_scatter(partial, 'dp', scatter_dimension=0, tiled=True)  62.3 us
    reduce_scatter x1, waiting for transfers between devices, body(): rows_out = lax.psum_scatter(term, 'tensor', scatter_dimension=0, tiled=True)  28 us
    dot_general x3, matrix products, summed(): partial = jnp.dot(gathered, weights, preferred_element_type=jnp.float32)  18.4 us
    all_gather x1, blocking collectives, body(): gathered = lax.all_gather(columns, 'tensor', axis=0, tiled=True)  16.2 us
    all_to_all x1, blocking collectives, body(): lax.all_to_all(tokens, 'dp', split_axis=1, concat_axis=0, tiled=True)  8.97 us
    all_gather x1, blocking collectives, body(): hidden_all = lax.all_gather(hidden_product, 'dp', axis=0, tiled=True)  8.74 us
    dot_general x1, matrix products, body(): jnp.dot(hidden_all, down_projection_matrix, preferred_element_type=jnp.fl...  7.51 us
    all_to_all x1, blocking collectives, body(): lax.all_to_all(rows_out.astype(jnp.bfloat16), 'dp', split_axis=0, concat_...  7.14 us
  transfers between devices with their start and end apart: 4, of which 4 were waited for; matrix products, arithmetic and copies ran while one was open for 11% of the time, Pallas kernels for 0%

commit v1 on v0

--- a/solution.py
+++ b/solution.py
@@ -4,6 +4,18 @@
 from jax.sharding import PartitionSpec as P
 
 adapter_scale_factor = 0.5
+
+
+def ring_gather(value, axis, dim):
+    ways, here, turn = (lax.axis_size(axis), lax.axis_index(axis), value.shape[dim])
+    shape = [n * ways if d == dim else n for d, n in enumerate(value.shape)]
+    full = lax.dynamic_update_slice_in_dim(
+        jnp.zeros(shape, value.dtype), value, here * turn, axis=dim
+    )
+    for far in range(1, ways):
+        value = lax.ppermute(value, axis, [(d, (d + 1) % ways) for d in range(ways)])
+        full = lax.dynamic_update_slice_in_dim(full, value, (here - far) % ways * turn, axis=dim)
+    return full
 
 
 def body(
@@ -20,7 +32,7 @@
 ):
     adapter_rank_size = gate_adapter_inmap.shape[1]
     columns = lax.all_to_all(tokens, "dp", split_axis=1, concat_axis=0, tiled=True)
-    gathered = lax.all_gather(columns, "tensor", axis=0, tiled=True)
+    gathered = ring_gather(columns, "tensor", 0)
 
     def summed(weights):
         partial = jnp.dot(gathered, weights, preferred_element_type=jnp.float32)

time: 182 us -> 183 us (level)
  blocking collectives: 41 us -> 15.9 us
  waiting for transfers between devices: 93.8 us -> 114 us
  starting transfers between devices: 0.13 us -> 6.61 us
  other arithmetic: 0.96 us -> 3.02 us
    ppermute x0 -> x3, waiting for transfers between devices: none -> 18.6 us  [ring_gather(): lax.ppermute(value, axis, [(d, (d + 1) % ways) for d in range(ways)])]
    all_gather x1 -> x0, blocking collectives: 16.2 us -> none  [body(): gathered = lax.all_gather(columns, 'tensor', axis=0, tiled=True)]
    all_to_all x1 -> x0, blocking collectives: 8.97 us -> none  [body(): lax.all_to_all(tokens, 'dp', split_axis=1, concat_axis=0, tiled=True)]
    all_to_all x0 -> x1, waiting for transfers between devices: none -> 4.6 us  [body(): lax.all_to_all(tokens, 'dp', split_axis=1, concat_axis=0, tiled=True)]
    all_to_all x0 -> x1, starting transfers between devices: none -> 4.37 us  [body(): lax.all_to_all(tokens, 'dp', split_axis=1, concat_axis=0, tiled=True)]
    unnamed x5 -> x4, waiting for transfers between devices: 3.5 us -> 0.07 us
    ppermute x0 -> x3, starting transfers between devices: none -> 2.12 us  [ring_gather(): lax.ppermute(value, axis, [(d, (d + 1) % ways) for d in range(ways)])]
    convert_element_type x0 -> x2, other arithmetic: none -> 2.05 us  [the longest x1 1.3 us: body(): (jax.nn.silu(gate_activated) * up_projected_value).astype(jnp.bfloat16)]
  transfers between devices with their start and end apart: 4 -> 8, of which waited for: 4 -> 7; matrix products, arithmetic and copies ran while one was open for 11% -> 10% of each run, Pallas kernels for 0% -> 0%
where the time goes in v1:
time: 183 us
  waiting for transfers between devices  114 us (62%)
  matrix products  29 us (16%)
  blocking collectives  15.9 us (9%)
  between operations  13.2 us (7%)
  starting transfers between devices  6.61 us (4%)
  other arithmetic  3.02 us (2%)
    reduce_scatter x3, waiting for transfers between devices, summed(): return lax.psum_scatter(partial, 'dp', scatter_dimension=0, tiled=True)  63 us
    reduce_scatter x1, waiting for transfers between devices, body(): rows_out = lax.psum_scatter(term, 'tensor', scatter_dimension=0, tiled=True)  28 us
    dot_general x3, matrix products, summed(): partial = jnp.dot(gathered, weights, preferred_element_type=jnp.float32)  19.1 us
    ppermute x3, waiting for transfers between devices, ring_gather(): lax.ppermute(value, axis, [(d, (d + 1) % ways) for d in range(ways)])  18.6 us
    all_gather x1, blocking collectives, body(): hidden_all = lax.all_gather(hidden_product, 'dp', axis=0, tiled=True)  8.74 us
    dot_general x1, matrix products, body(): jnp.dot(hidden_all, down_projection_matrix, preferred_element_type=jnp.fl...  7.51 us
    all_to_all x1, blocking collectives, body(): lax.all_to_all(rows_out.astype(jnp.bfloat16), 'dp', split_axis=0, concat_...  7.14 us
    all_to_all x1, waiting for transfers between devices, body(): lax.all_to_all(tokens, 'dp', split_axis=1, concat_axis=0, tiled=True)  4.6 us
  transfers between devices with their start and end apart: 8, of which 7 were waited for; matrix products, arithmetic and copies ran while one was open for 10% of the time, Pallas kernels for 0%

profile of v1, /device:TPU:0, one launch (start us, length us, event | category | flops | bytes accessed | tf_op | source)
XLA Modules:
  0.0 182.7 jit_solution(447606287409007583)
XLA Ops:
  6.5 0.0 copy-start
  6.5 4.4 %all-to-all-start = ((bf16[8,4,2048]{2,0,1:T(8,128)(2,1)}), bf16[8,4,2048]{2,0,1:T(8,128)(2,1)S(1)}, u32[]{:S(2)}, u32[]{:S(2)}) async-start(bf16[8,4,2048]{2,0,1:T(8,128)(2,1)} %bitcast.24), calls=%async_computation | async-start | bytes 262144 | tf_op jit(solution)/shard_map/all_to_all | solution.py:34
  10.9 0.0 reduce-scatter.7.cloned.1.call-start
  10.9 4.6 %all-to-all-done = bf16[8,4,2048]{2,0,1:T(8,128)(2,1)S(1)} async-done(((bf16[8,4,2048]{2,0,1:T(8,128)(2,1)}), bf16[8,4,2048]{2,0,1:T(8,128)(2,1)S(1)}, u32[]{:S(2)}, u32[]{:S(2)}) %all-to-all-start) | async-done | bytes 131104 | tf_op jit(solution)/shard_map/all_to_all | solution.py:34
  15.5 2.1 %collective-permute-start = (bf16[32,2048]{1,0:T(8,128)(2,1)S(1)}, bf16[32,2048]{1,0:T(8,128)(2,1)S(1)}, u32[]{:S(2)}, u32[]{:S(2)}) collective-permute-start(bf16[32,2048]{1,0:T(8,128)(2,1)S(1)} %bitcast.22), channel_id=1, source_target_pairs={{0,4},{4,8},{8,12},{12,0},{1,5},{5,9},{9,13},{13,1},{2,6},{6,10},{... | collective-permute-start | bytes 393224 | tf_op jit(solution)/shard_map/ppermute | solution.py:16
  17.7 5.1 %collective-permute-done = bf16[32,2048]{1,0:T(8,128)(2,1)S(1)} collective-permute-done((bf16[32,2048]{1,0:T(8,128)(2,1)S(1)}, bf16[32,2048]{1,0:T(8,128)(2,1)S(1)}, u32[]{:S(2)}, u32[]{:S(2)}) %collective-permute-start) | collective-permute-done | bytes 131104 | tf_op jit(solution)/shard_map/ppermute | solution.py:16
  22.8 0.0 collective-permute-start.1
  22.8 6.7 %collective-permute-done.1 = bf16[32,2048]{1,0:T(8,128)(2,1)S(1)} collective-permute-done((bf16[32,2048]{1,0:T(8,128)(2,1)S(1)}, bf16[32,2048]{1,0:T(8,128)(2,1)S(1)}, u32[]{:S(2)}, u32[]{:S(2)}) %collective-permute-start.1) | collective-permute-done | bytes 131104 | tf_op jit(solution)/shard_map/ppermute | solution.py:16
  29.5 0.0 collective-permute-start.2
  29.6 6.7 %collective-permute-done.2 = bf16[32,2048]{1,0:T(8,128)(2,1)S(1)} collective-permute-done((bf16[32,2048]{1,0:T(8,128)(2,1)S(1)}, bf16[32,2048]{1,0:T(8,128)(2,1)S(1)}, u32[]{:S(2)}, u32[]{:S(2)}) %collective-permute-start.2) | collective-permute-done | bytes 131104 | tf_op jit(solution)/shard_map/ppermute | solution.py:16
  36.3 2.0 %fusion.1 = f32[128,128]{1,0:T(8,128)} fusion(bf16[128,2048]{1,0:T(8,128)(2,1)S(1)} %constant_dynamic-update-slice_fusion, bf16[2048,64]{0,1:T(8,128)(2,1)} %param.16, bf16[2048,64]{0,1:T(8,128)(2,1)} %param.14), kind=kOutput, calls=%fused_computation.4 | convolution fusion | flops 68157440 | bytes 1114112 | tf_op jit(solution)/shard_map/dot_general | solution.py:38
  38.3 0.0 reduce-scatter.7.cloned.1.call-update
  38.3 0.0 reduce-scatter.5.cloned.1.call-start
  38.4 8.6 %fusion.10 = f32[128,3584]{1,0:T(8,128)} fusion(bf16[128,2048]{1,0:T(8,128)(2,1)S(1)} %constant_dynamic-update-slice_fusion, bf16[2048,3584]{1,0:T(8,128)(2,1)} %param.11), kind=kOutput, calls=%fused_computation.19 | convolution fusion | flops 1879048192 | bytes 17039360 | tf_op jit(solution)/shard_map/dot_general | solution.py:38
  46.9 0.0 copy-start.1
  46.9 0.0 copy-start.2
  46.9 0.0 reduce-scatter.5.cloned.1.call-update
  46.9 0.0 reduce-scatter.9.cloned.1.call-start
  47.0 8.6 %fusion.11 = f32[128,3584]{1,0:T(8,128)} fusion(bf16[128,2048]{1,0:T(8,128)(2,1)S(1)} %constant_dynamic-update-slice_fusion, bf16[2048,3584]{1,0:T(8,128)(2,1)} %param.12), kind=kOutput, calls=%fused_computation.20 | convolution fusion | flops 1879048192 | bytes 17039360 | tf_op jit(solution)/shard_map/dot_general | solution.py:38
  55.6 0.0 copy-start.3
  55.6 0.0 reduce-scatter.9.cloned.1.call-update
  55.6 0.0 reduce-scatter.11.cloned.1.call-start
  55.6 0.0 reduce-scatter.7.cloned.1.call-done
  55.7 0.8 convert_element_type.10
  56.4 0.0 copy-done.1
  56.4 0.3 convolution_multiply_fusion
  56.7 0.0 copy-done.2
  56.7 0.2 convolution_multiply_fusion.1
  56.9 30.8 %reduce-scatter.5.cloned.1.call-done = f32[32,3584]{1,0:T(8,128)} async-done(((f32[128,3584]{1,0:T(8,128)}), f32[32,3584]{1,0:T(8,128)}) %reduce-scatter.5.cloned.1.call-update) | async-done | bytes 458768 | tf_op jit(solution)/shard_map/reduce_scatter | solution.py:39
  87.7 32.2 %reduce-scatter.9.cloned.1.call-done = f32[32,3584]{1,0:T(8,128)} async-done(((f32[128,3584]{1,0:T(8,128)}), f32[32,3584]{1,0:T(8,128)}) %reduce-scatter.9.cloned.1.call-update) | async-done | bytes 458768 | tf_op jit(solution)/shard_map/reduce_scatter | solution.py:39
  119.9 1.3 multiply_convert_fusion
  121.2 8.7 %all_gather.3 = bf16[128,3584]{1,0:T(8,128)(2,1)S(1)} all-gather(bf16[32,3584]{1,0:T(8,128)(2,1)S(1)} %multiply_convert_fusion), channel_id=1, replica_groups=mesh['groups'=2,'tensor'=4,'dp'=4] {'dp'}, dimensions={0}, use_global_device_ids=true | all-gather | bytes 1146880 | tf_op jit(solution)/shard_map/all_gather | solution.py:55
  129.9 7.5 %fusion.12 = f32[128,2048]{1,0:T(8,128)S(1)} fusion(bf16[128,3584]{1,0:T(8,128)(2,1)S(1)} %all_gather.3, bf16[3584,2048]{1,0:T(8,128)(2,1)} %param.13), kind=kOutput, calls=%fused_computation.21 | convolution fusion | flops 1879048192 | bytes 16646144 | tf_op jit(solution)/shard_map/dot_general | solution.py:61
  137.5 0.0 copy-done.3
  137.5 0.4 fusion.13
  137.9 0.0 copy-done
  137.9 1.6 fusion
  139.4 0.0 reduce-scatter.11.cloned.1.call-update
  139.5 28.0 %reduce-scatter.11.cloned.1.call-done = f32[32,2048]{1,0:T(8,128)} async-done(((f32[128,2048]{1,0:T(8,128)}), f32[32,2048]{1,0:T(8,128)}) %reduce-scatter.11.cloned.1.call-update) | async-done | bytes 262160 | tf_op jit(solution)/shard_map/reduce_scatter | solution.py:63
  167.4 1.0 convert_bitcast_fusion
  168.4 7.1 %all_to_all.38 = bf16[4,8,2048]{2,1,0:T(8,128)(2,1)S(1)} all-to-all(bf16[4,8,2048]{2,1,0:T(8,128)(2,1)S(1)} %convert_bitcast_fusion), channel_id=1, replica_groups=mesh['groups'=2,'tensor'=4,'dp'=4] {'dp'}, dimensions={0} | all-to-all | bytes 262144 | tf_op jit(solution)/shard_map/all_to_all | solution.py:64
  175.5 0.7 copy.16
  (5 shorter events, 0.1 us)
Async XLA Ops:
  6.5 131.3 %copy-start = (bf16[64,8192]{1,0:T(8,128)(2,1)S(1)}, bf16[64,8192]{1,0:T(8,128)(2,1)}, u32[]{:S(2)}) copy-start(bf16[64,8192]{1,0:T(8,128)(2,1)} %param.19) | copy-start | bytes 3145732
  6.5 9.0 %all-to-all-start = ((bf16[8,4,2048]{2,0,1:T(8,128)(2,1)}), bf16[8,4,2048]{2,0,1:T(8,128)(2,1)S(1)}, u32[]{:S(2)}, u32[]{:S(2)}) async-start(bf16[8,4,2048]{2,0,1:T(8,128)(2,1)} %bitcast.24), calls=%async_computation | async-start | bytes 262144 | tf_op jit(solution)/shard_map/all_to_all | solution.py:34
  10.9 44.8 %reduce-scatter.7.cloned.1.call-start = ((), (), s32[]{:S(2)}) async-start(), calls=%async_computation.7 | async-start | bytes 81920 | tf_op jit(solution)/shard_map/reduce_scatter | solution.py:39
  15.5 7.3 %collective-permute-start = (bf16[32,2048]{1,0:T(8,128)(2,1)S(1)}, bf16[32,2048]{1,0:T(8,128)(2,1)S(1)}, u32[]{:S(2)}, u32[]{:S(2)}) collective-permute-start(bf16[32,2048]{1,0:T(8,128)(2,1)S(1)} %bitcast.22), channel_id=1, source_target_pairs={{0,4},{4,8},{8,12},{12,0},{1,5},{5,9},{9,13},{13,1},{2,6},{6,10},{... | collective-permute-start | bytes 393224 | tf_op jit(solution)/shard_map/ppermute | solution.py:16
  22.8 6.8 %collective-permute-start.1 = (bf16[32,2048]{1,0:T(8,128)(2,1)S(1)}, bf16[32,2048]{1,0:T(8,128)(2,1)S(1)}, u32[]{:S(2)}, u32[]{:S(2)}) collective-permute-start(bf16[32,2048]{1,0:T(8,128)(2,1)S(1)} %collective-permute-done), channel_id=1, source_target_pairs={{0,4},{4,8},{8,12},{12,0},{1,5},{5,9},{9,13},{13,1},{2,6},{6,10},{... | collective-permute-start | bytes 393224 | tf_op jit(solution)/shard_map/ppermute | solution.py:16
  29.5 6.8 %collective-permute-start.2 = (bf16[32,2048]{1,0:T(8,128)(2,1)S(1)}, bf16[32,2048]{1,0:T(8,128)(2,1)S(1)}, u32[]{:S(2)}, u32[]{:S(2)}) collective-permute-start(bf16[32,2048]{1,0:T(8,128)(2,1)S(1)} %collective-permute-done.1), channel_id=1, source_target_pairs={{0,4},{4,8},{8,12},{12,0},{1,5},{5,9},{9,13},{13,1},{2,6},{6,10},{... | collective-permute-start | bytes 393224 | tf_op jit(solution)/shard_map/ppermute | solution.py:16
  38.3 49.4 %reduce-scatter.5.cloned.1.call-start = ((), (), s32[]{:S(2)}) async-start(), calls=%async_computation.6 | async-start | bytes 2293760 | tf_op jit(solution)/shard_map/reduce_scatter | solution.py:39
  46.9 9.5 %copy-start.1 = (bf16[64,3584]{1,0:T(8,128)(2,1)S(1)}, bf16[64,3584]{1,0:T(8,128)(2,1)}, u32[]{:S(2)}) copy-start(bf16[64,3584]{1,0:T(8,128)(2,1)} %param.17) | copy-start | bytes 1376260
  46.9 9.8 %copy-start.2 = (bf16[64,3584]{1,0:T(8,128)(2,1)S(1)}, bf16[64,3584]{1,0:T(8,128)(2,1)}, u32[]{:S(2)}) copy-start(bf16[64,3584]{1,0:T(8,128)(2,1)} %param.15) | copy-start | bytes 1376260
  46.9 73.0 %reduce-scatter.9.cloned.1.call-start = ((), (), s32[]{:S(2)}) async-start(), calls=%async_computation.8 | async-start | bytes 2293760 | tf_op jit(solution)/shard_map/reduce_scatter | solution.py:39
  55.6 81.9 %copy-start.3 = (bf16[3584,64]{0,1:T(8,128)(2,1)S(1)}, bf16[3584,64]{0,1:T(8,128)(2,1)}, u32[]{:S(2)}) copy-start(bf16[3584,64]{0,1:T(8,128)(2,1)} %param.18) | copy-start | bytes 1376260
  55.6 111.8 %reduce-scatter.11.cloned.1.call-start = ((), (), s32[]{:S(2)}) async-start(), calls=%async_computation.9 | async-start | bytes 1310720 | tf_op jit(solution)/shard_map/reduce_scatter | solution.py:63
Sparse Core Ops, SparseCore 0:
  38.4 17.1 reduce-scatter.6
  58.1 29.5 reduce-scatter.4
  90.3 29.5 reduce-scatter.8
  139.6 27.8 reduce-scatter.10
